TPU v7x, 128 devices: a whole 4x4x4 slice. The times are simulated.
128 devices in a mesh: group: 8 (over x_lo, z), tensor: 16 (over x_hi, y, core).
Axes of the slice: x: 4 (x_hi: 2, x_lo: 2; x = x_hi * 2 + x_lo), y: 4, z: 4, core: 2. Of those that a mesh axis runs over, the one named last changes fastest.
Arguments:
- hidden: bfloat16 [12288, 2048], P(('group', 'tensor')), may hold values from -20 to 20
- request_of: int32 [12288], P('group'), may hold values from 0 to 191, as said below
- positions: int32 [12288], P('group'), may hold values from 0 to 511, as said below
- page_table: int32 [8, 64], P('group'), may hold values from 0 to 63, each once within a row
- attn_gain: float32 [2048], replicated, may hold values from 0.5 to 1.5
- mlp_gain: float32 [2048], replicated, may hold values from 0.5 to 1.5
- wq: float32 [2048, 2048], P('group', 'tensor'), may hold values from -2 to 2
- wk: float32 [2048, 1024], P('group', 'tensor'), may hold values from -1 to 1
- wv: float32 [2048, 1024], P('group', 'tensor'), may hold values from -0.125 to 0.125
- wo: float32 [2048, 2048], P('tensor', 'group'), may hold values from -0.125 to 0.125
- w_gate: float32 [2048, 8192], P('group', 'tensor'), may hold values from -0.125 to 0.125
- w_up: float32 [2048, 8192], P('group', 'tensor'), may hold values from -0.125 to 0.125
- w_down: float32 [8192, 2048], P('tensor', 'group'), may hold values from -0.0625 to 0.0625
Outputs:
- layer_out: bfloat16 [12288, 2048], P(('group', 'tensor'))
- kv_pages: bfloat16 [512, 128, 2048], P('group', None, 'tensor')
Inputs may be any that keep to these rules, and one draw needn't show every extreme that they name: `request_of`: prompt numbers rise strictly along the token stream, starting at 0, and the last prompt of the stream has the number 12288 // 64 - 1; a prompt's rows are consecutive, and a prompt that reaches the last row of one block of 1536 rows continues at the first row of the next block. A prompt's rows have positions 0, 1, 2 and so on in order; a prompt has at most 512 rows, and one has exactly 512.
All inputs are finite; a program needn't handle non-finite values.
Results may differ from a plain program's by a relative error of at most 0.014.
Values may be sent and summed in bfloat16 or wider, within the bound.
A program may use at most 128 MiB of HBM per device.

v0:
```python
import jax
import jax.numpy as jnp
from jax import lax
from jax.sharding import PartitionSpec as P

QH = 16
KVH = 8
HD = 128
PAGE = 128
rope_base = 1000000.0
norm_eps = 1e-06


def partner(value, axis, distance):
    mask = 2**distance
    pairs = [(source, source ^ mask) for source in range(lax.axis_size(axis))]
    return lax.ppermute(value, axis, pairs)


def from_behind(block, axis, distance):
    devices = range(lax.axis_size(axis))
    route = [(i - distance, i) for i in devices if i - distance in devices]
    return lax.ppermute(block, axis, route)


def rms_scale(values, gain):
    square = jnp.mean(values * values, axis=-1, keepdims=True)
    return (values * lax.rsqrt(square + norm_eps) * gain).astype(jnp.bfloat16)


def rotate(values, places):
    half_dim = values.shape[-1] // 2
    frequency = rope_base ** (-(jnp.arange(half_dim, dtype=jnp.float32) * 2.0 / values.shape[-1]))
    angle = places.astype(jnp.float32)[:, None] * frequency[None, :]
    cosine = jnp.cos(angle)[:, None, :]
    sine = jnp.sin(angle)[:, None, :]
    widened = values.astype(jnp.float32)
    first = widened[..., :half_dim]
    second = widened[..., half_dim:]
    return jnp.concatenate(
        [first * cosine - second * sine, second * cosine + first * sine], axis=-1
    ).astype(jnp.bfloat16)


def join_halves(own_part, other_part):
    even = lax.axis_index("tensor") % 2 == 0
    lower = jnp.where(even, own_part, other_part)
    upper = jnp.where(even, other_part, own_part)
    return jnp.concatenate([lower, upper], axis=-1)


def contract_rows(acts, pieces):
    return tuple((jnp.dot(acts, piece, preferred_element_type=jnp.float32) for piece in pieces))


def body(
    hidden,
    request_of,
    positions,
    page_table,
    attn_gain,
    mlp_gain,
    wq,
    wk,
    wv,
    wo,
    w_gate,
    w_up,
    w_down,
):
    tensor_count = lax.axis_size("tensor")
    rows_dev = hidden.shape[0]
    tok_group = request_of.shape[0]
    query_heads = QH // tensor_count
    key_heads = max(1, KVH // tensor_count)
    group_ratio = QH // KVH
    residual = lax.all_gather(hidden, "tensor", axis=0, tiled=True).astype(jnp.float32)
    normed = rms_scale(residual, attn_gain)
    query_rows = wq.astype(jnp.bfloat16)
    key_rows = wk.astype(jnp.bfloat16)
    value_rows = wv.astype(jnp.bfloat16)
    other_key, other_value = partner((key_rows, value_rows), "tensor", 0)
    key_rows = join_halves(key_rows, other_key)
    value_rows = join_halves(value_rows, other_value)
    query_sum, key_sum, value_sum = contract_rows(
        normed,
        (
            lax.all_gather(query_rows, "group", axis=0, tiled=True),
            lax.all_gather(key_rows, "group", axis=0, tiled=True),
            lax.all_gather(value_rows, "group", axis=0, tiled=True),
        ),
    )
    query_raw = query_sum.astype(jnp.bfloat16)
    key_raw = key_sum.astype(jnp.bfloat16)
    value_raw = value_sum.astype(jnp.bfloat16)
    queries = rotate(query_raw.reshape(tok_group, query_heads, HD), positions)
    keys = rotate(key_raw.reshape(tok_group, key_heads, HD), positions)
    values = value_raw.reshape(tok_group, key_heads, HD)
    kv_rows = jnp.stack([keys, values], axis=2)
    earlier = from_behind(kv_rows, "group", 1)
    earlier_rows = earlier.shape[0]
    all_rows = jnp.concatenate([earlier, kv_rows], axis=0)
    all_keys = jnp.repeat(all_rows[:, :, 0], group_ratio, axis=1)[:, :query_heads]
    all_values = jnp.repeat(all_rows[:, :, 1], group_ratio, axis=1)[:, :query_heads]
    first_request = request_of[0]
    first_position = positions[0]
    same_local = (request_of[:, None] == request_of[None, :]) & (
        positions[None, :] <= positions[:, None]
    )
    same_earlier = (request_of[:, None] == first_request) & (
        jnp.arange(earlier_rows)[None, :] >= earlier_rows - first_position
    )
    visible = jnp.concatenate([same_earlier, same_local], axis=1)
    scores = jnp.einsum(
        "qhd,khd->hqk", queries, all_keys, preferred_element_type=jnp.float32
    ) * HD ** (-0.5)
    scores = jnp.where(visible[None], scores, -1e30)
    row_peak = jnp.max(scores, axis=-1, keepdims=True)
    probs = jnp.where(visible[None], jnp.exp(scores - row_peak), 0.0)
    total = jnp.sum(probs, axis=-1, keepdims=True)
    mixed_heads = jnp.einsum(
        "hqk,khd->qhd", probs.astype(jnp.bfloat16), all_values, preferred_element_type=jnp.float32
    ) / jnp.transpose(total, (1, 0, 2))
    attended = mixed_heads.astype(jnp.bfloat16).reshape(tok_group, query_heads * HD)
    out_rows = wo.astype(jnp.bfloat16)
    attn_part = jnp.dot(
        attended,
        lax.all_gather(out_rows, "group", axis=1, tiled=True),
        preferred_element_type=jnp.float32,
    )
    mixed = residual + lax.psum(attn_part.astype(jnp.bfloat16), "tensor").astype(jnp.float32)
    normed_mlp = rms_scale(mixed, mlp_gain)
    gate_rows = w_gate.astype(jnp.bfloat16)
    up_rows = w_up.astype(jnp.bfloat16)
    gate_sum, up_sum = contract_rows(
        normed_mlp,
        (
            lax.all_gather(gate_rows, "group", axis=0, tiled=True),
            lax.all_gather(up_rows, "group", axis=0, tiled=True),
        ),
    )
    activation = (jax.nn.silu(gate_sum) * up_sum).astype(jnp.bfloat16)
    down_rows = w_down.astype(jnp.bfloat16)
    down_part = jnp.dot(
        activation,
        lax.all_gather(down_rows, "group", axis=1, tiled=True),
        preferred_element_type=jnp.float32,
    )
    summed = lax.psum(down_part.astype(jnp.bfloat16), "tensor").astype(jnp.float32)
    first_row = lax.axis_index("tensor") * rows_dev
    own_mixed = lax.dynamic_slice_in_dim(mixed, first_row, rows_dev, 0)
    own_summed = lax.dynamic_slice_in_dim(summed, first_row, rows_dev, 0)
    layer_out = (own_mixed + own_summed).astype(jnp.bfloat16)
    pages = page_table.shape[1]
    changed = jnp.concatenate(
        [jnp.ones((1,), jnp.int32), (request_of[1:] != request_of[:-1]).astype(jnp.int32)]
    )
    opens = jnp.maximum(changed, (positions % PAGE == 0).astype(jnp.int32))
    logical = jnp.cumsum(opens) - 1
    chosen = jnp.sum(
        jnp.where(logical[:, None] == jnp.arange(pages)[None, :], page_table, 0), axis=1
    )
    target = chosen * PAGE + positions % PAGE
    width = 2 * KVH * HD // tensor_count
    flat_rows = kv_rows.reshape(tok_group, key_heads * 2 * HD)
    offset = lax.axis_index("tensor") * width % (key_heads * 2 * HD)
    own_slice = lax.dynamic_slice_in_dim(flat_rows, offset, width, 1)
    cache = jnp.zeros((pages * PAGE, width), jnp.bfloat16).at[target].set(own_slice)
    return (layer_out, cache.reshape(pages, PAGE, width))


def solution(mesh):
    placed = (
        P(("group", "tensor"), None),
        P("group"),
        P("group"),
        P("group", None),
        P(),
        P(),
        P("group", "tensor"),
        P("group", "tensor"),
        P("group", "tensor"),
        P("tensor", "group"),
        P("group", "tensor"),
        P("group", "tensor"),
        P("tensor", "group"),
    )
    return jax.shard_map(
        body,
        mesh=mesh,
        in_specs=placed,
        out_specs=(P(("group", "tensor"), None), P("group", None, "tensor")),
        check_vma=False,
    )
```

profile of v0, /device:TPU:0, one launch (start us, length us, event | category | flops | bytes accessed | tf_op | source)
XLA Modules:
  0.0 593.4 jit_solution(9900236413319749413)
XLA Ops:
  8.1 0.7 all-gather.5.cloned.1.call-update
  8.8 0.8 convert_element_type.103
  9.6 0.8 convert_element_type.108
  10.5 0.5 collective-permute-start.1
  11.0 0.9 convert_element_type.110
  11.9 1.2 slice.43
  13.1 1.2 slice.42
  14.3 0.8 slice_compare_fusion
  15.2 0.8 maximum_bitcast_fusion
  15.9 0.3 reduce-window.9
  16.3 0.9 convert_element_type.117
  17.9 0.1 slice_reduce_fusion
  18.1 0.8 select_reduce_fusion
  18.9 1.4 iota_compare_fusion.1
  20.2 0.8 compare_select_fusion
  21.0 30.5 %all_gather.27 = bf16[2048,128]{1,0:T(8,128)(2,1)S(1)} all-gather(bf16[256,128]{1,0:T(8,128)(2,1)S(1)} %convert_element_type.110), channel_id=1, replica_groups=mesh['group'=8,'tensor'=16] {'group'}, dimensions={0}, use_global_device_ids=true | all-gather | bytes 589824 | tf_op jit(solution)/shard_map/all_gather | solution.py:88
  51.6 32.5 %all_gather.28 = bf16[128,2048]{1,0:T(8,128)(2,1)} all-gather(bf16[128,256]{1,0:T(8,128)(2,1)S(1)} %convert_element_type.117), channel_id=1, replica_groups=mesh['group'=8,'tensor'=16] {'group'}, dimensions={1}, use_global_device_ids=true | all-gather | bytes 589824 | tf_op jit(solution)/shard_map/all_gather | solution.py:128
  84.0 3.3 compare_and_fusion
  87.5 29.4 %all_gather.25 = bf16[2048,128]{0,1:T(8,128)(2,1)S(1)} all-gather(bf16[256,128]{0,1:T(8,128)(2,1)S(1)} %pad_maximum_fusion.1), channel_id=1, replica_groups=mesh['group'=8,'tensor'=16] {'group'}, dimensions={0}, use_global_device_ids=true | all-gather | bytes 589824 | tf_op jit(solution)/shard_map/all_gather | solution.py:89
  116.8 30.9 %all_gather.26 = bf16[2048,128]{0,1:T(8,128)(2,1)} all-gather(bf16[256,128]{0,1:T(8,128)(2,1)S(1)} %pad_maximum_fusion.2), channel_id=1, replica_groups=mesh['group'=8,'tensor'=16] {'group'}, dimensions={0}, use_global_device_ids=true | all-gather | bytes 589824 | tf_op jit(solution)/shard_map/all_gather | solution.py:90
  147.7 4.2 fusion.1
  152.0 0.3 copy-done
  152.3 1.5 fusion.3
  153.8 2.2 fusion.13
  156.0 2.2 fusion.16
  158.3 2.2 fusion.14
  160.5 1.7 fusion.52
  162.3 4.2 collective-permute-start.2
  166.5 1.5 broadcast_and_fusion
  168.1 7.7 %collective-permute-done.2 = bf16[1536,1,2,128]{0,3,2,1:T(8,128)(2,1)S(1)} collective-permute-done((bf16[1536,1,2,128]{0,3,2,1:T(8,128)(2,1)S(1)}, bf16[1536,1,2,128]{0,3,2,1:T(8,128)(2,1)S(1)}, u32[]{:S(2)}, u32[]{:S(2)}) %collective-permute-start.2) | collective-permute-done | bytes 786464 | tf_op jit(solution)/shard_map/ppermute | solution.py:23
  175.8 0.2 maximum_maximum_fusion
  176.0 4.1 fusion
  180.1 6.4 %copy-done.1 = f32[1536,3072]{1,0:T(8,128)} copy-done((f32[1536,3072]{1,0:T(8,128)}, f32[1536,3072]{1,0:T(8,128)S(1)}, u32[]{:S(2)}) %copy-start.1) | copy-done | bytes 18874392
  186.5 6.4 %fusion.4 = f32[1536]{0:T(1024)S(1)} fusion(f32[1536,3072]{1,0:T(8,128)S(1)} %get-tuple-element.17, f32[1536]{0:T(1024)S(1)} %get-tuple-element.16, pred[1536,1536]{1,0:T(32,128)(4,1)S(1)} %compare_and_fusion, pred[1536,1536]{1,0:T(32,128)(4,1)S(1)} %broadcast_and_fusion), kind=kLoop, calls=%fused_computation.13 | loop fusion | flops 28310016 | bytes 23605248 | tf_op jit(solution)/shard_map/reduce_sum | solution.py:120
  192.9 14.1 %convolution_convert_fusion.1 = bf16[1536,2048]{1,0:T(8,128)(2,1)} fusion(bf16[128,2048]{1,0:T(8,128)(2,1)} %all_gather.28, f32[1536,3072]{1,0:T(8,128)} %copy-done.1, f32[1536]{0:T(1024)S(1)} %get-tuple-element.16, bf16[3072,1,2,128]{0,3,2,1:T(8,128)(2,1)} %copy-done.3, f32[1536]{0:T(1024)S(1)} %fusion.4, pred[1536,1536]{1,0:T(32,128)(4,1)S(1)} %compare_and_fusion, ...), kind=kOutput, calls=%fused_computation.18 | convolution fusion | flops 2045116416 | bytes 31207424 | tf_op jit(solution)/shard_map/dot_general | solution.py:126
  207.1 1.0 copy-done.4
  208.1 0.8 convert_element_type.121
  208.9 0.7 convert_element_type.124
  209.7 0.7 convert_element_type.122
  210.5 0.3 all-reduce.5.cloned.1.call-start
  210.8 179.3 %all-reduce.3.cloned.1.call-done = bf16[1536,2048]{1,0:T(8,128)(2,1)} async-done(((bf16[1536,2048]{1,0:T(8,128)(2,1)}), bf16[1536,2048]{1,0:T(8,128)(2,1)}) %all-reduce.3.cloned.1.call-update) | async-done | bytes 6291472 | tf_op jit(solution)/shard_map/psum | solution.py:131
  390.1 11.2 %multiply_reduce_fusion = (f32[1536]{0:T(1024)S(1)}, f32[1536,2048]{1,0:T(8,128)}) fusion(bf16[1536,2048]{1,0:T(8,128)(2,1)} %all-reduce.3.cloned.1.call-done, bf16[1536,2048]{1,0:T(8,128)(2,1)} %all-gather.5.cloned.1.call-done), kind=kLoop, calls=%fused_computation.12 | loop fusion | flops 15727104 | bytes 25171968 | tf_op jit(solution)/shard_map/reduce_sum | solution.py:27
  401.3 10.4 %fusion.64 = f32[1536,512]{1,0:T(8,128)} fusion(bf16[2048,512]{1,0:T(8,128)(2,1)} %all-gather.7.cloned.1.call-done, f32[2048]{0:T(1024)S(1)} %copy-done.11, f32[1536]{0:T(1024)S(1)} %add_rsqrt_fusion, bf16[1536,2048]{1,0:T(8,128)(2,1)} %all-gather.5.cloned.1.call-done, bf16[1536,2048]{1,0:T(8,128)(2,1)} %all-reduce.3.cloned.1.call-done), kind=kOutput, calls=%fused_computation.96 | convolution fusion | flops 3240099840 | bytes 17840128 | tf_op jit(solution)/shard_map/dot_general | solution.py:53
  411.7 15.3 %convolution_convert_fusion = bf16[1536,2048]{1,0:T(8,128)(2,1)} fusion(bf16[512,2048]{1,0:T(8,128)(2,1)} %all-gather.11.cloned.1.call-done, bf16[2048,512]{1,0:T(8,128)(2,1)} %all-gather.9.cloned.1.call-done, f32[1536,512]{1,0:T(8,128)} %fusion.64, f32[2048]{0:T(1024)S(1)} %copy-done.11, f32[1536]{0:T(1024)S(1)} %add_rsqrt_fusion, ...), kind=kOutput, calls=%fused_computation.17 | convolution fusion | flops 6469189632 | bytes 26228736 | tf_op jit(solution)/shard_map/dot_general | solution.py:144
  427.1 0.2 copy.17
  427.3 6.1 %scatter_custom_fusion = bf16[8192,128]{1,0:T(8,128)(2,1)} fusion(s32[1536]{0:T(1024)S(1)} %get-tuple-element.14, bf16[1536,128]{1,0:T(8,128)(2,1)S(1)} %copy.17, bf16[]{:T(256)} %constant.84.clone.1), kind=kCustom, calls=%fused_computation.35 | custom fusion | bytes 2097154 | tf_op jit(solution)/shard_map/scatter | solution.py:168
  433.4 150.6 %all-reduce.5.cloned.1.call-done = bf16[1536,2048]{1,0:T(8,128)(2,1)} async-done(((bf16[1536,2048]{1,0:T(8,128)(2,1)}), bf16[1536,2048]{1,0:T(8,128)(2,1)}) %all-reduce.5.cloned.1.call-update) | async-done | bytes 6291472 | tf_op jit(solution)/shard_map/psum | solution.py:149
  584.0 2.1 add_convert_fusion
  (49 shorter events, 0.7 us)
Async XLA Ops:
  8.0 79.4 %copy-start.9 = (f32[256,64]{0,1:T(8,128)S(1)}, f32[256,64]{0,1:T(8,128)}, u32[]{:S(2)}) copy-start(f32[256,64]{0,1:T(8,128)} %param.20) | copy-start | bytes 196612
  8.0 79.4 %copy-start.8 = (f32[256,64]{0,1:T(8,128)S(1)}, f32[256,64]{0,1:T(8,128)}, u32[]{:S(2)}) copy-start(f32[256,64]{0,1:T(8,128)} %param.21) | copy-start | bytes 196612
  8.0 139.7 %all-gather.5.cloned.1.call-start = ((), (), s32[]{:S(2)}) async-start(), calls=%async_computation | async-start | bytes 6684672 | tf_op jit(solution)/shard_map/all_gather | solution.py:77
  8.8 381.3 %all-reduce.3.cloned.1.call-start = ((), (), s32[]{:S(2)}) async-start(), calls=%async_computation.1 | async-start | bytes 12582912 | tf_op jit(solution)/shard_map/psum | solution.py:131
  9.6 77.7 %collective-permute-start = (bf16[256,64]{0,1:T(8,128)(2,1)S(1)}, bf16[256,64]{0,1:T(8,128)(2,1)S(1)}, u32[]{:S(2)}, u32[]{:S(2)}) collective-permute-start(bf16[256,64]{0,1:T(8,128)(2,1)S(1)} %convert_element_type.103), channel_id=1, source_target_pairs={{0,1},{1,0},{2,3},{3,2},{4,5},{5,4},{6,7},{7,6},{8,9},{9,8},{10,11... | collective-permute-start | bytes 98312 | tf_op jit(solution)/shard_map/ppermute | solution.py:17
  10.5 76.9 %collective-permute-start.1 = (bf16[256,64]{0,1:T(8,128)(2,1)S(1)}, bf16[256,64]{0,1:T(8,128)(2,1)S(1)}, u32[]{:S(2)}, u32[]{:S(2)}) collective-permute-start(bf16[256,64]{0,1:T(8,128)(2,1)S(1)} %convert_element_type.108), channel_id=1, source_target_pairs={{0,1},{1,0},{2,3},{3,2},{4,5},{5,4},{6,7},{7,6},{8,9},{9,8},{10,11... | collective-permute-start | bytes 98312 | tf_op jit(solution)/shard_map/ppermute | solution.py:17
  84.0 67.9 %copy-start.10 = (f32[2048]{0:T(1024)S(1)}, f32[2048]{0:T(1024)}, u32[]{:S(2)}) copy-start(f32[2048]{0:T(1024)} %param.17) | copy-start | bytes 24580
  147.7 4.6 copy-start
  156.0 2.2 copy-start.7
  162.3 13.5 %collective-permute-start.2 = (bf16[1536,1,2,128]{0,3,2,1:T(8,128)(2,1)S(1)}, bf16[1536,1,2,128]{0,3,2,1:T(8,128)(2,1)S(1)}, u32[]{:S(2)}, u32[]{:S(2)}) collective-permute-start(bf16[1536,1,2,128]{0,3,2,1:T(8,128)(2,1)S(1)} %pad_maximum_fusion), channel_id=1, source_target_pairs={{0,16},{16,32},{32,48},{48,64},{64,80},{80,96},{96,112},{1,17},{17... | collective-permute-start | bytes 2359304 | tf_op jit(solution)/shard_map/ppermute | solution.py:23
  168.1 12.0 %copy-start.2 = (pred[1536,1536]{1,0:T(32,128)(4,1)}, pred[1536,1536]{1,0:T(32,128)(4,1)S(1)}, u32[]{:S(2)}) copy-start(pred[1536,1536]{1,0:T(32,128)(4,1)S(1)} %broadcast_and_fusion) | copy-start | bytes 7077892
  176.0 4.1 copy-start.3
  180.1 6.5 %copy-start.1 = (f32[1536,3072]{1,0:T(8,128)}, f32[1536,3072]{1,0:T(8,128)S(1)}, u32[]{:S(2)}) copy-start(f32[1536,3072]{1,0:T(8,128)S(1)} %get-tuple-element.17) | copy-start | bytes 56623108
  207.0 1.0 copy-start.4
  207.0 1.9 copy-start.5
  207.0 2.7 copy-start.6
  207.1 194.2 %all-gather.7.cloned.1.call-start = ((), (), s32[]{:S(2)}) async-start(), calls=%async_computation.2 | async-start | bytes 2359296 | tf_op jit(solution)/shard_map/all_gather | solution.py:138
  208.8 202.8 %all-gather.11.cloned.1.call-start = ((), (), s32[]{:S(2)}) async-start(), calls=%async_computation.4 | async-start | bytes 2359296 | tf_op jit(solution)/shard_map/all_gather | solution.py:146
  209.7 202.0 %all-gather.9.cloned.1.call-start = ((), (), s32[]{:S(2)}) async-start(), calls=%async_computation.3 | async-start | bytes 2359296 | tf_op jit(solution)/shard_map/all_gather | solution.py:139
  210.5 190.8 %copy-start.11 = (f32[2048]{0:T(1024)S(1)}, f32[2048]{0:T(1024)}, u32[]{:S(2)}) copy-start(f32[2048]{0:T(1024)} %param.18) | copy-start | bytes 24580
  210.5 373.5 %all-reduce.5.cloned.1.call-start = ((), (), s32[]{:S(2)}) async-start(), calls=%async_computation.5 | async-start | bytes 12582912 | tf_op jit(solution)/shard_map/psum | solution.py:149
Sparse Core Ops, SparseCore 0:
  11.3 70.2 all-gather.4
  207.2 182.8 all-reduce.2
  427.1 156.8 all-reduce.4
Sparse Core Ops, SparseCore 1:
  209.2 49.1 all-gather.6
  260.3 41.6 all-gather.10
  304.1 50.6 all-gather.8
where the time goes:
time: 594 us; the launch traced here: 593 us
  waiting for transfers between devices  338 us (57%)
  blocking collectives  123 us (21%)
  matrix products  50.5 us (9%)
  other arithmetic  42.9 us (7%)
  local copies, waits for them, and re-layouts  16.7 us (3%)
  between operations  16.4 us (3%)
    psum x1, waiting for transfers between devices, body(): lax.psum(attn_part.astype(jnp.bfloat16), 'tensor').astype(jnp.float32)  179 us
    psum x1, waiting for transfers between devices, body(): lax.psum(down_part.astype(jnp.bfloat16), 'tensor').astype(jnp.float32)  151 us
    all_gather x1, blocking collectives, body(): lax.all_gather(out_rows, 'group', axis=1, tiled=True)  32.5 us
    all_gather x1, blocking collectives, body(): lax.all_gather(value_rows, 'group', axis=0, tiled=True)  30.9 us
    all_gather x1, blocking collectives, body(): lax.all_gather(query_rows, 'group', axis=0, tiled=True)  30.5 us
    all_gather x1, blocking collectives, body(): lax.all_gather(key_rows, 'group', axis=0, tiled=True)  29.4 us
    dot_general x4, matrix products, contract_rows(): jnp.dot(acts, piece, preferred_element_type=jnp.float32)  17 us
    reduce_sum x2, other arithmetic, rms_scale(): square = jnp.mean(values * values, axis=-1, keepdims=True)  15.4 us
  transfers between devices with their start and end apart: 9, of which 3 were waited for; matrix products, arithmetic and copies ran while one was open for 8% of the time, Pallas kernels for 0%

commit v1 on v0

--- a/solution.py
+++ b/solution.py
@@ -86,7 +86,10 @@
         normed,
         (
             lax.all_gather(query_rows, "group", axis=0, tiled=True),
-            lax.all_gather(key_rows, "group", axis=0, tiled=True),
+            jnp.concatenate(
+                lax.all_to_all(jnp.stack([key_rows] * lax.axis_size("group")), "group", 0, 0),
+                axis=0,
+            ),
             lax.all_gather(value_rows, "group", axis=0, tiled=True),
         ),
     )

time: 594 us -> 578 us (0.973)
  blocking collectives: 123 us -> 96.5 us
    all_gather x1 -> x0, blocking collectives: 29.4 us -> none  [body(): lax.all_gather(key_rows, 'group', axis=0, tiled=True)]
  transfers between devices with their start and end apart: 9 -> 10, of which waited for: 3 -> 3; matrix products, arithmetic and copies ran while one was open for 8% -> 10% of each run, Pallas kernels for 0% -> 0%
where the time goes in v1:
time: 578 us
  waiting for transfers between devices  340 us (59%)
  blocking collectives  96.5 us (17%)
  matrix products  53.5 us (9%)
  other arithmetic  45.5 us (8%)
  local copies, waits for them, and re-layouts  17.7 us (3%)
  between operations  16.4 us (3%)
  starting transfers between devices  8.22 us (1%)
    psum x1, waiting for transfers between devices, body(): lax.psum(attn_part.astype(jnp.bfloat16), 'tensor').astype(jnp.float32)  181 us
    psum x1, waiting for transfers between devices, body(): lax.psum(down_part.astype(jnp.bfloat16), 'tensor').astype(jnp.float32)  151 us
    all_gather x1, blocking collectives, body(): lax.all_gather(value_rows, 'group', axis=0, tiled=True)  33.5 us
    all_gather x1, blocking collectives, body(): lax.all_gather(out_rows, 'group', axis=1, tiled=True)  32.5 us
    all_gather x1, blocking collectives, body(): lax.all_gather(query_rows, 'group', axis=0, tiled=True)  30.5 us
    dot_general x4, matrix products, contract_rows(): jnp.dot(acts, piece, preferred_element_type=jnp.float32)  20 us
    reduce_sum x2, other arithmetic, rms_scale(): square = jnp.mean(values * values, axis=-1, keepdims=True)  15.4 us
    dot_general x1, matrix products, body(): jnp.dot(activation, lax.all_gather(down_rows, 'group', axis=1, tiled=True...  15.4 us
  transfers between devices with their start and end apart: 10, of which 3 were waited for; matrix products, arithmetic and copies ran while one was open for 10% of the time, Pallas kernels for 0%

profile of v1, /device:TPU:0, one launch (start us, length us, event | category | flops | bytes accessed | tf_op | source)
XLA Modules:
  0.0 577.7 jit_solution(3232758222370022637)
XLA Ops:
  8.1 0.7 all-gather.5.cloned.1.call-update
  8.8 0.8 convert_element_type.103
  9.6 0.8 convert_element_type.108
  10.4 0.5 collective-permute-start.1
  11.0 0.9 convert_element_type.110
  11.9 1.2 slice.43
  13.1 1.2 slice.42
  14.3 0.8 slice_compare_fusion
  15.1 0.8 maximum_bitcast_fusion
  15.9 0.3 reduce-window.9
  16.3 0.9 convert_element_type.117
  18.0 0.8 select_reduce_fusion
  18.8 1.4 iota_compare_fusion.1
  20.2 0.8 compare_select_fusion
  21.0 30.5 %all_gather.23 = bf16[2048,128]{1,0:T(8,128)(2,1)S(1)} all-gather(bf16[256,128]{1,0:T(8,128)(2,1)S(1)} %convert_element_type.110), channel_id=1, replica_groups=mesh['group'=8,'tensor'=16] {'group'}, dimensions={0}, use_global_device_ids=true | all-gather | bytes 589824 | tf_op jit(solution)/shard_map/all_gather | solution.py:88
  51.4 32.5 %all_gather.24 = bf16[128,2048]{1,0:T(8,128)(2,1)} all-gather(bf16[128,256]{1,0:T(8,128)(2,1)S(1)} %convert_element_type.117), channel_id=1, replica_groups=mesh['group'=8,'tensor'=16] {'group'}, dimensions={1}, use_global_device_ids=true | all-gather | bytes 589824 | tf_op jit(solution)/shard_map/all_gather | solution.py:131
  84.0 3.3 compare_and_fusion
  87.5 0.9 stack.4
  88.4 5.6 all-to-all-start
  94.1 33.5 %all_gather.22 = bf16[2048,128]{0,1:T(8,128)(2,1)} all-gather(bf16[256,128]{0,1:T(8,128)(2,1)S(1)} %pad_maximum_fusion.2), channel_id=1, replica_groups=mesh['group'=8,'tensor'=16] {'group'}, dimensions={0}, use_global_device_ids=true | all-gather | bytes 589824 | tf_op jit(solution)/shard_map/all_gather | solution.py:93
  127.5 4.2 fusion.1
  131.8 0.3 copy-done.1
  132.1 4.1 fusion.3
  136.2 5.2 fusion.13
  141.4 2.2 fusion.16
  143.7 2.2 fusion.14
  145.9 1.7 fusion.52
  147.7 1.6 collective-permute-start.2
  149.3 1.5 broadcast_and_fusion
  150.9 7.7 %collective-permute-done.2 = bf16[1536,1,2,128]{0,3,2,1:T(8,128)(2,1)S(1)} collective-permute-done((bf16[1536,1,2,128]{0,3,2,1:T(8,128)(2,1)S(1)}, bf16[1536,1,2,128]{0,3,2,1:T(8,128)(2,1)S(1)}, u32[]{:S(2)}, u32[]{:S(2)}) %collective-permute-start.2) | collective-permute-done | bytes 786464 | tf_op jit(solution)/shard_map/ppermute | solution.py:23
  158.6 0.2 maximum_maximum_fusion
  158.8 4.1 fusion
  162.9 6.4 %copy-done.2 = f32[1536,3072]{1,0:T(8,128)} copy-done((f32[1536,3072]{1,0:T(8,128)}, f32[1536,3072]{1,0:T(8,128)S(1)}, u32[]{:S(2)}) %copy-start.2) | copy-done | bytes 18874392
  169.3 6.4 %fusion.4 = f32[1536]{0:T(1024)S(1)} fusion(f32[1536,3072]{1,0:T(8,128)S(1)} %get-tuple-element.17, f32[1536]{0:T(1024)S(1)} %get-tuple-element.16, pred[1536,1536]{1,0:T(32,128)(4,1)S(1)} %compare_and_fusion, pred[1536,1536]{1,0:T(32,128)(4,1)S(1)} %broadcast_and_fusion), kind=kLoop, calls=%fused_computation.13 | loop fusion | flops 28310016 | bytes 23605248 | tf_op jit(solution)/shard_map/reduce_sum | solution.py:123
  175.7 14.1 %convolution_convert_fusion.1 = bf16[1536,2048]{1,0:T(8,128)(2,1)} fusion(bf16[128,2048]{1,0:T(8,128)(2,1)} %all_gather.24, f32[1536,3072]{1,0:T(8,128)} %copy-done.2, f32[1536]{0:T(1024)S(1)} %get-tuple-element.16, bf16[3072,1,2,128]{0,3,2,1:T(8,128)(2,1)} %copy-done.4, f32[1536]{0:T(1024)S(1)} %fusion.4, pred[1536,1536]{1,0:T(32,128)(4,1)S(1)} %compare_and_fusion, ...), kind=kOutput, calls=%fused_computation.18 | convolution fusion | flops 2045116416 | bytes 31207424 | tf_op jit(solution)/shard_map/dot_general | solution.py:129
  189.9 1.0 copy-done.5
  190.9 0.7 convert_element_type.121
  191.7 0.7 convert_element_type.124
  192.5 0.7 convert_element_type.122
  193.3 0.3 all-reduce.5.cloned.1.call-start
  193.5 180.5 %all-reduce.3.cloned.1.call-done = bf16[1536,2048]{1,0:T(8,128)(2,1)} async-done(((bf16[1536,2048]{1,0:T(8,128)(2,1)}), bf16[1536,2048]{1,0:T(8,128)(2,1)}) %all-reduce.3.cloned.1.call-update) | async-done | bytes 6291472 | tf_op jit(solution)/shard_map/psum | solution.py:134
  374.1 11.2 %multiply_reduce_fusion = (f32[1536]{0:T(1024)S(1)}, f32[1536,2048]{1,0:T(8,128)}) fusion(bf16[1536,2048]{1,0:T(8,128)(2,1)} %all-reduce.3.cloned.1.call-done, bf16[1536,2048]{1,0:T(8,128)(2,1)} %all-gather.5.cloned.1.call-done), kind=kLoop, calls=%fused_computation.12 | loop fusion | flops 15727104 | bytes 25171968 | tf_op jit(solution)/shard_map/reduce_sum | solution.py:27
  385.3 10.4 %fusion.64 = f32[1536,512]{1,0:T(8,128)} fusion(bf16[2048,512]{1,0:T(8,128)(2,1)} %all-gather.7.cloned.1.call-done, f32[2048]{0:T(1024)S(1)} %copy-done.12, f32[1536]{0:T(1024)S(1)} %add_rsqrt_fusion, bf16[1536,2048]{1,0:T(8,128)(2,1)} %all-gather.5.cloned.1.call-done, bf16[1536,2048]{1,0:T(8,128)(2,1)} %all-reduce.3.cloned.1.call-done), kind=kOutput, calls=%fused_computation.96 | convolution fusion | flops 3240099840 | bytes 17840128 | tf_op jit(solution)/shard_map/dot_general | solution.py:53
  395.7 15.4 %convolution_convert_fusion = bf16[1536,2048]{1,0:T(8,128)(2,1)} fusion(bf16[512,2048]{1,0:T(8,128)(2,1)} %all-gather.11.cloned.1.call-done, bf16[2048,512]{1,0:T(8,128)(2,1)} %all-gather.9.cloned.1.call-done, f32[1536,512]{1,0:T(8,128)} %fusion.64, f32[2048]{0:T(1024)S(1)} %copy-done.12, f32[1536]{0:T(1024)S(1)} %add_rsqrt_fusion, ...), kind=kOutput, calls=%fused_computation.17 | convolution fusion | flops 6469189632 | bytes 26228736 | tf_op jit(solution)/shard_map/dot_general | solution.py:147
  411.1 0.2 copy.20
  411.4 6.1 %scatter_custom_fusion = bf16[8192,128]{1,0:T(8,128)(2,1)} fusion(s32[1536]{0:T(1024)S(1)} %get-tuple-element.14, bf16[1536,128]{1,0:T(8,128)(2,1)S(1)} %copy.20, bf16[]{:T(256)} %constant.84.clone.1), kind=kCustom, calls=%fused_computation.35 | custom fusion | bytes 2097154 | tf_op jit(solution)/shard_map/scatter | solution.py:171
  417.5 150.8 %all-reduce.5.cloned.1.call-done = bf16[1536,2048]{1,0:T(8,128)(2,1)} async-done(((bf16[1536,2048]{1,0:T(8,128)(2,1)}), bf16[1536,2048]{1,0:T(8,128)(2,1)}) %all-reduce.5.cloned.1.call-update) | async-done | bytes 6291472 | tf_op jit(solution)/shard_map/psum | solution.py:152
  568.3 2.1 add_convert_fusion
  (54 shorter events, 0.9 us)
Async XLA Ops:
  8.0 79.3 %copy-start.10 = (f32[256,64]{0,1:T(8,128)S(1)}, f32[256,64]{0,1:T(8,128)}, u32[]{:S(2)}) copy-start(f32[256,64]{0,1:T(8,128)} %param.20) | copy-start | bytes 196612
  8.0 79.3 %copy-start.9 = (f32[256,64]{0,1:T(8,128)S(1)}, f32[256,64]{0,1:T(8,128)}, u32[]{:S(2)}) copy-start(f32[256,64]{0,1:T(8,128)} %param.21) | copy-start | bytes 196612
  8.0 119.5 %all-gather.5.cloned.1.call-start = ((), (), s32[]{:S(2)}) async-start(), calls=%async_computation.1 | async-start | bytes 6684672 | tf_op jit(solution)/shard_map/all_gather | solution.py:77
  9.6 77.7 %collective-permute-start = (bf16[256,64]{0,1:T(8,128)(2,1)S(1)}, bf16[256,64]{0,1:T(8,128)(2,1)S(1)}, u32[]{:S(2)}, u32[]{:S(2)}) collective-permute-start(bf16[256,64]{0,1:T(8,128)(2,1)S(1)} %convert_element_type.103), channel_id=1, source_target_pairs={{0,1},{1,0},{2,3},{3,2},{4,5},{5,4},{6,7},{7,6},{8,9},{9,8},{10,11... | collective-permute-start | bytes 98312 | tf_op jit(solution)/shard_map/ppermute | solution.py:17
  10.4 76.9 %collective-permute-start.1 = (bf16[256,64]{0,1:T(8,128)(2,1)S(1)}, bf16[256,64]{0,1:T(8,128)(2,1)S(1)}, u32[]{:S(2)}, u32[]{:S(2)}) collective-permute-start(bf16[256,64]{0,1:T(8,128)(2,1)S(1)} %convert_element_type.108), channel_id=1, source_target_pairs={{0,1},{1,0},{2,3},{3,2},{4,5},{5,4},{6,7},{7,6},{8,9},{9,8},{10,11... | collective-permute-start | bytes 98312 | tf_op jit(solution)/shard_map/ppermute | solution.py:17
  87.3 44.5 %copy-start.11 = (f32[2048]{0:T(1024)S(1)}, f32[2048]{0:T(1024)}, u32[]{:S(2)}) copy-start(f32[2048]{0:T(1024)} %param.17) | copy-start | bytes 24580
  88.4 47.9 %all-to-all-start = ((bf16[8,256,128]{2,1,0:T(8,128)(2,1)}), bf16[8,256,128]{2,1,0:T(8,128)(2,1)S(1)}, u32[]{:S(2)}, u32[]{:S(2)}) async-start(bf16[8,256,128]{2,1,0:T(8,128)(2,1)} %stack.4), calls=%async_computation | async-start | bytes 1048576 | tf_op jit(solution)/shard_map/all_to_all | solution.py:90
  94.0 280.1 %all-reduce.3.cloned.1.call-start = ((), (), s32[]{:S(2)}) async-start(), calls=%async_computation.2 | async-start | bytes 12582912 | tf_op jit(solution)/shard_map/psum | solution.py:134
  127.5 4.6 copy-start.1
  136.2 5.2 copy-start
  141.4 2.2 copy-start.8
  147.7 10.9 %collective-permute-start.2 = (bf16[1536,1,2,128]{0,3,2,1:T(8,128)(2,1)S(1)}, bf16[1536,1,2,128]{0,3,2,1:T(8,128)(2,1)S(1)}, u32[]{:S(2)}, u32[]{:S(2)}) collective-permute-start(bf16[1536,1,2,128]{0,3,2,1:T(8,128)(2,1)S(1)} %pad_maximum_fusion), channel_id=1, source_target_pairs={{0,16},{16,32},{32,48},{48,64},{64,80},{80,96},{96,112},{1,17},{17... | collective-permute-start | bytes 2359304 | tf_op jit(solution)/shard_map/ppermute | solution.py:23
  150.9 12.0 %copy-start.3 = (pred[1536,1536]{1,0:T(32,128)(4,1)}, pred[1536,1536]{1,0:T(32,128)(4,1)S(1)}, u32[]{:S(2)}) copy-start(pred[1536,1536]{1,0:T(32,128)(4,1)S(1)} %broadcast_and_fusion) | copy-start | bytes 7077892
  158.8 4.1 copy-start.4
  162.9 6.5 %copy-start.2 = (f32[1536,3072]{1,0:T(8,128)}, f32[1536,3072]{1,0:T(8,128)S(1)}, u32[]{:S(2)}) copy-start(f32[1536,3072]{1,0:T(8,128)S(1)} %get-tuple-element.17) | copy-start | bytes 56623108
  189.8 1.0 copy-start.5
  189.8 1.9 copy-start.6
  189.8 2.7 copy-start.7
  189.9 195.4 %all-gather.7.cloned.1.call-start = ((), (), s32[]{:S(2)}) async-start(), calls=%async_computation.3 | async-start | bytes 2359296 | tf_op jit(solution)/shard_map/all_gather | solution.py:141
  191.6 204.1 %all-gather.11.cloned.1.call-start = ((), (), s32[]{:S(2)}) async-start(), calls=%async_computation.5 | async-start | bytes 2359296 | tf_op jit(solution)/shard_map/all_gather | solution.py:149
  192.4 203.3 %all-gather.9.cloned.1.call-start = ((), (), s32[]{:S(2)}) async-start(), calls=%async_computation.4 | async-start | bytes 2359296 | tf_op jit(solution)/shard_map/all_gather | solution.py:142
  193.3 192.0 %copy-start.12 = (f32[2048]{0:T(1024)S(1)}, f32[2048]{0:T(1024)}, u32[]{:S(2)}) copy-start(f32[2048]{0:T(1024)} %param.18) | copy-start | bytes 24580
  193.3 375.1 %all-reduce.5.cloned.1.call-start = ((), (), s32[]{:S(2)}) async-start(), calls=%async_computation.6 | async-start | bytes 12582912 | tf_op jit(solution)/shard_map/psum | solution.py:152
Sparse Core Ops, SparseCore 0:
  11.3 70.2 all-gather.4
  190.0 184.0 all-reduce.2
  411.2 157.0 all-reduce.4
Sparse Core Ops, SparseCore 1:
  192.0 50.1 all-gather.6
  244.2 41.2 all-gather.10
  287.5 50.4 all-gather.8
